TPU v7x, 32 devices: a whole 2x2x4 slice. The times are simulated.
32 devices in a mesh: groups: 2 (over x), day: 16 (over z, y, core).
Axes of the slice: x: 2, y: 2, z: 4, core: 2. Of those that a mesh axis runs over, the one named last changes fastest.
Arguments:
- couplings: float32 [6, 128, 32, 512], P(None, ('groups', 'day')), parts along dimension 1, may hold values from 0.01 to 2.7, as said below
- probe_bits: int32 [16, 128, 32, 512], P(None, ('groups', 'day')), parts along dimension 1, may hold values 0 or 1
- land_mask: int32 [64, 512], P('groups'), parts along dimension 0, may hold values 0 or 1
Outputs:
- variance: float32 [128, 32, 512], P(('groups', 'day')), parts along dimension 0
There are 2 independent parts, one for each index of `groups`. A program takes and returns all parts, laid end to end along the dimension named above; each array names one. Nothing has to cross between parts.
Inputs may be any that keep to these rules, and one draw needn't show every extreme that they name: `couplings`: all weights positive.
All inputs are finite; a program needn't handle non-finite values. No bound on the sum of `probe_bits` on one device may be relied on, other than what follows from the above.
Results may differ from a plain program's by a relative error of at most 0.0003.
Values sent between devices are 32-bit elements; how exact they have to be, the bound alone decides.
No kernel may reach another device: no remote copies, remote signals or barrier semaphores. Data moves between devices by JAX's collectives and lax.ppermute only.
A program may use at most 64 MiB of HBM per device.

v0:
```python
import jax
import jax.numpy as jnp
from jax import lax
from jax.sharding import PartitionSpec as P

ITERS = 3
LINK_OFFSETS = ((0, 1), (1, 0), (1, 1), (1, -1))
COASTAL_FACTOR = 0.2


def passed_along(value, axis, steps):
    count = lax.axis_size(axis)
    pairs = [(source, (source + steps) % count) for source in range(count)]
    return lax.ppermute(value, axis, pairs)


def extended(block, sides, width):
    for axis, dim in sides:
        count = lax.axis_size(axis)
        forward = [(i, i + 1) for i in range(count - 1)]
        forward.append((count - 1, 0))
        backward = [(target, source) for source, target in forward]
        low = lax.ppermute(
            lax.slice_in_dim(block, block.shape[dim] - width, None, axis=dim), axis, forward
        )
        high = lax.ppermute(lax.slice_in_dim(block, 0, width, axis=dim), axis, backward)
        block = jnp.concatenate([low, block, high], axis=dim)
    return block


def shift_plane(values, step_row, step_col):
    lat_size, lon_size = (values.shape[-2], values.shape[-1])
    margins = [(0, 0)] * (values.ndim - 2) + [
        (max(step_row, 0), max(-step_row, 0)),
        (max(step_col, 0), max(-step_col, 0)),
    ]
    padded = jnp.pad(values, margins)
    row_start = max(-step_row, 0)
    col_start = max(-step_col, 0)
    return padded[..., row_start : row_start + lat_size, col_start : col_start + lon_size]


def prepare(couplings, land_mask):
    ones_field = jnp.ones(land_mask.shape, jnp.float32)
    result = [couplings[0]]
    for slot_n, (step_row, step_col) in enumerate(LINK_OFFSETS):
        target = shift_plane(land_mask, -step_row, -step_col)
        inside = shift_plane(ones_field, -step_row, -step_col)
        factor = (
            jnp.where(land_mask == target, jnp.float32(1.0), jnp.float32(COASTAL_FACTOR)) * inside
        )
        result.append(couplings[slot_n + 1] * factor)
    result.append(couplings[5])
    return jnp.stack(result)


def stencil(padded, coef_block, link_prev):
    field = padded[..., 1:-1, :, :]
    next_day = padded[..., 2:, :, :]
    prev_day = padded[..., :-2, :, :]
    result = (
        coef_block[0] * field + coef_block[5] * (field - next_day) + link_prev * (field - prev_day)
    )
    for slot_n, (step_row, step_col) in enumerate(LINK_OFFSETS):
        link_coef = coef_block[slot_n + 1]
        link_back = shift_plane(link_coef, step_row, step_col)
        result = result + link_coef * (field - shift_plane(field, -step_row, -step_col))
        result = result + link_back * (field - shift_plane(field, step_row, step_col))
    return result


def diagonal(coef_block, link_prev):
    result = coef_block[0] + coef_block[5] + link_prev
    for slot_n, (step_row, step_col) in enumerate(LINK_OFFSETS):
        link_coef = coef_block[slot_n + 1]
        result = result + link_coef + shift_plane(link_coef, step_row, step_col)
    return result


def spread(vector):
    return vector[:, None, None, None]


def summed(first, second):
    return jnp.sum(first * second, axis=(1, 2, 3))


def norm_sum(residual, scaled):
    return lax.psum(summed(residual, scaled), "day")


def body(couplings, probe_bits, land_mask):
    probes_n, days_n = (probe_bits.shape[0], probe_bits.shape[1])
    links_eff = prepare(couplings, land_mask)
    signs = (2 * probe_bits - 1).astype(jnp.float32)
    prev_plane = passed_along(links_eff[5, days_n - 1 : days_n], "day", 1)
    link_prev = jnp.concatenate([prev_plane, links_eff[5, : days_n - 1]], axis=0)
    diag_own = diagonal(links_eff, link_prev)
    residual = signs
    scaled = signs / diag_own
    estimate = jnp.zeros_like(signs)
    norm_now = norm_sum(residual, scaled)
    direction = scaled
    for turn in range(ITERS):
        padded = extended(direction, (("day", 1),), 1)
        image = stencil(padded, links_eff, link_prev)
        step_len = norm_now / lax.psum(summed(direction, image), "day")
        estimate = estimate + spread(step_len) * direction
        if turn + 1 < ITERS:
            residual = residual - spread(step_len) * image
            scaled = residual / diag_own
            norm_next = norm_sum(residual, scaled)
            direction = scaled + spread(norm_next / norm_now) * direction
            norm_now = norm_next
    return jnp.sum(signs * estimate, axis=0) / probes_n


def solution(mesh):
    return jax.shard_map(
        body,
        mesh=mesh,
        in_specs=(
            P(None, ("groups", "day"), None, None),
            P(None, ("groups", "day"), None, None),
            P("groups", None),
        ),
        out_specs=P(("groups", "day"), None, None),
        check_vma=False,
    )
```

profile of v0, /device:TPU:0, one launch (start us, length us, event | category | flops | bytes accessed | tf_op | source)
XLA Modules:
  0.0 300.4 jit_solution(4284825563196142856)
XLA Ops:
  0.0 0.0 copy-start
  0.0 1.0 slice_bitcast_fusion.3
  1.0 0.5 collective-permute-start
  1.5 1.2 fusion.93
  2.7 1.3 bitcast_multiply_fusion.3
  4.0 0.9 slice_bitcast_fusion.2
  4.9 3.5 %collective-permute-done = f32[1,32,512]{2,1,0:T(8,128)S(1)} collective-permute-done((f32[1,32,512]{2,1,0:T(8,128)S(1)}, f32[1,32,512]{2,1,0:T(8,128)S(1)}, u32[]{:S(2)}, u32[]{:S(2)}) %collective-permute-start) | collective-permute-done | bytes 65568 | tf_op jit(solution)/shard_map/ppermute | solution.py:14
  8.4 1.5 pad_maximum_fusion.6
  9.9 0.0 copy-done
  9.9 0.9 convert_divide_fusion
  10.8 0.0 copy-start.3
  10.9 0.2 fusion.104
  11.0 1.8 collective-permute-start.1
  12.9 0.0 collective-permute-start.2
  12.9 0.0 copy-done.3
  12.9 0.2 slice_bitcast_fusion.1
  13.1 12.1 %collective-permute-done.1 = f32[16,1,32,512]{3,2,1,0:T(8,128)S(1)} collective-permute-done((f32[16,1,32,512]{3,2,1,0:T(8,128)S(1)}, f32[16,1,32,512]{3,2,1,0:T(8,128)S(1)}, u32[]{:S(2)}, u32[]{:S(2)}) %collective-permute-start.1) | collective-permute-done | bytes 1048608 | tf_op jit(solution)/shard_map/ppermute | solution.py:26
  25.2 4.7 %collective-permute-done.2 = f32[16,1,32,512]{3,2,1,0:T(8,128)S(1)} collective-permute-done((f32[16,1,32,512]{3,2,1,0:T(8,128)S(1)}, f32[16,1,32,512]{3,2,1,0:T(8,128)S(1)}, u32[]{:S(2)}, u32[]{:S(2)}) %collective-permute-start.2) | collective-permute-done | bytes 1048608 | tf_op jit(solution)/shard_map/ppermute | solution.py:23
  29.9 12.8 %multiply_reduce_fusion.4 = (f32[16]{0:T(128)S(1)}, f32[16]{0:T(128)S(1)}, f32[16,4,32,512]{3,2,1,0:T(8,128)}) fusion(f32[4,32,512]{2,1,0:T(8,128)S(1)} %get-tuple-element.31, s32[16,4,32,512]{3,2,1,0:T(8,128)S(1)} %copy-done, f32[16,4,32,512]{3,2,1,0:T(8,128)S(1)} %convert_divide_fusion, f32[4,32,512]{2,1,0:T(8,128)S(1)} %get-tuple-element.35, ...), kind=kLoop, calls=%fused_computation.129 | loop fusion | flops 42991584 | bytes 17825920 | tf_op jit(solution)/shard_map/reduce_sum | solution.py:85
  42.7 35.4 %all-reduce.36 = (f32[16]{0:T(128)S(1)}, f32[16]{0:T(128)S(1)}) all-reduce(f32[16]{0:T(128)S(1)} %get-tuple-element.6, f32[16]{0:T(128)S(1)} %get-tuple-element.5), channel_id=1, replica_groups=mesh['groups'=2,'day'=16] {'day'}, use_global_device_ids=true, to_apply=%region_1.2 | all-reduce | flops 32 | bytes 256 | tf_op jit(solution)/shard_map/psum | solution.py:89
  78.1 6.6 %multiply_reduce_fusion.3 = (f32[16]{0:T(128)S(1)}, f32[16,4,32,512]{3,2,1,0:T(8,128)}) fusion(f32[4,32,512]{2,1,0:T(8,128)S(1)} %get-tuple-element.31, f32[16,4,32,512]{3,2,1,0:T(8,128)} %get-tuple-element.13, f32[16]{0:T(128)S(1)} %div.43, s32[16,4,32,512]{3,2,1,0:T(8,128)} %param.4), kind=kLoop, calls=%fused_computation.127 | loop fusion | flops 8388592 | bytes 12845184 | tf_op jit(solution)/shard_map/reduce_sum | solution.py:85
  84.7 29.6 %psum.44 = f32[16]{0:T(128)S(1)} all-reduce(f32[16]{0:T(128)S(1)} %get-tuple-element.11), channel_id=1, replica_groups=mesh['groups'=2,'day'=16] {'day'}, use_global_device_ids=true, to_apply=%region_5.6 | all-reduce | flops 16 | bytes 128 | tf_op jit(solution)/shard_map/psum | solution.py:89
  114.4 4.6 %multiply_add_fusion.1 = f32[16,4,32,512]{3,2,1,0:T(8,128)S(1)} fusion(f32[16,4,32,512]{3,2,1,0:T(8,128)} %get-tuple-element.12, f32[16]{0:T(128)S(1)} %div.45, f32[4,32,512]{2,1,0:T(8,128)S(1)} %get-tuple-element.31, s32[16,4,32,512]{3,2,1,0:T(8,128)} %param.4), kind=kLoop, calls=%fused_computation.126 | loop fusion | flops 7340032 | bytes 12845120 | tf_op jit(solution)/shard_map/add | solution.py:113
  119.0 0.0 copy-start.1
  119.0 0.3 fusion.103
  119.3 0.1 collective-permute-start.3
  119.4 0.5 collective-permute-start.4
  119.9 11.8 %collective-permute-done.3 = f32[16,1,32,512]{3,2,1,0:T(8,128)S(1)} collective-permute-done((f32[16,1,32,512]{3,2,1,0:T(8,128)S(1)}, f32[16,1,32,512]{3,2,1,0:T(8,128)S(1)}, u32[]{:S(2)}, u32[]{:S(2)}) %collective-permute-start.3) | collective-permute-done | bytes 1048608 | tf_op jit(solution)/shard_map/ppermute | solution.py:26
  131.7 4.8 %collective-permute-done.4 = f32[16,1,32,512]{3,2,1,0:T(8,128)S(1)} collective-permute-done((f32[16,1,32,512]{3,2,1,0:T(8,128)S(1)}, f32[16,1,32,512]{3,2,1,0:T(8,128)S(1)}, u32[]{:S(2)}, u32[]{:S(2)}) %collective-permute-start.4) | collective-permute-done | bytes 1048608 | tf_op jit(solution)/shard_map/ppermute | solution.py:23
  136.5 12.2 %multiply_reduce_fusion.2 = (f32[16]{0:T(128)S(1)}, f32[16,4,32,512]{3,2,1,0:T(8,128)}) fusion(f32[16,4,32,512]{3,2,1,0:T(8,128)S(1)} %multiply_add_fusion.1, f32[4,32,512]{2,1,0:T(8,128)S(1)} %get-tuple-element.35, f32[4,32,512]{2,1,0:T(8,128)S(1)} %get-tuple-element.24, f32[4,32,512]{2,1,0:T(8,128)S(1)} %get-tuple-element.34, ...), kind=kLoop, calls=%fused_computation.125 | loop fusion | flops 36700144 | bytes 13369408 | tf_op jit(solution)/shard_map/reduce_sum | solution.py:85
  148.7 0.0 copy-done.1
  148.7 37.5 %psum.45 = f32[16]{0:T(128)S(1)} all-reduce(f32[16]{0:T(128)S(1)} %get-tuple-element.9), channel_id=1, replica_groups=mesh['groups'=2,'day'=16] {'day'}, use_global_device_ids=true, to_apply=%region_7.8 | all-reduce | flops 16 | bytes 128 | tf_op jit(solution)/shard_map/psum | solution.py:107
  186.3 4.4 %multiply_reduce_fusion.1 = f32[16]{0:T(128)S(1)} fusion(f32[4,32,512]{2,1,0:T(8,128)S(1)} %get-tuple-element.31, f32[16,4,32,512]{3,2,1,0:T(8,128)} %get-tuple-element.12, f32[16,4,32,512]{3,2,1,0:T(8,128)} %get-tuple-element.10, f32[16]{0:T(128)S(1)} %div.46), kind=kLoop, calls=%fused_computation.123 | loop fusion | flops 5242864 | bytes 8650880 | tf_op jit(solution)/shard_map/reduce_sum | solution.py:85
  190.7 29.5 %psum.46 = f32[16]{0:T(128)S(1)} all-reduce(f32[16]{0:T(128)S(1)} %multiply_reduce_fusion.1), channel_id=1, replica_groups=mesh['groups'=2,'day'=16] {'day'}, use_global_device_ids=true, to_apply=%region_9.10 | all-reduce | flops 16 | bytes 128 | tf_op jit(solution)/shard_map/psum | solution.py:89
  220.2 6.4 %multiply_add_fusion = f32[16,4,32,512]{3,2,1,0:T(8,128)S(1)} fusion(f32[16,4,32,512]{3,2,1,0:T(8,128)} %copy-done.1, f32[16]{0:T(128)S(1)} %div.48, f32[4,32,512]{2,1,0:T(8,128)S(1)} %get-tuple-element.31, f32[16,4,32,512]{3,2,1,0:T(8,128)} %get-tuple-element.12, f32[16,4,32,512]{3,2,1,0:T(8,128)} %get-tuple-element.10, f32[16]{0:T(128)S(1)} %div.46), kind=kLoop, calls=%fused_computation.122 | loop fusion | flops 5242880 | bytes 17039488 | tf_op jit(solution)/shard_map/add | solution.py:113
  226.6 0.0 copy-start.2
  226.6 0.3 fusion.102
  226.9 0.1 collective-permute-start.5
  227.0 0.5 collective-permute-start.6
  227.5 11.8 %collective-permute-done.5 = f32[16,1,32,512]{3,2,1,0:T(8,128)S(1)} collective-permute-done((f32[16,1,32,512]{3,2,1,0:T(8,128)S(1)}, f32[16,1,32,512]{3,2,1,0:T(8,128)S(1)}, u32[]{:S(2)}, u32[]{:S(2)}) %collective-permute-start.5) | collective-permute-done | bytes 1048608 | tf_op jit(solution)/shard_map/ppermute | solution.py:26
  239.3 4.9 %collective-permute-done.6 = f32[16,1,32,512]{3,2,1,0:T(8,128)S(1)} collective-permute-done((f32[16,1,32,512]{3,2,1,0:T(8,128)S(1)}, f32[16,1,32,512]{3,2,1,0:T(8,128)S(1)}, u32[]{:S(2)}, u32[]{:S(2)}) %collective-permute-start.6) | collective-permute-done | bytes 1048608 | tf_op jit(solution)/shard_map/ppermute | solution.py:23
  244.2 0.0 copy-done.2
  244.2 11.4 %fusion.91 = f32[16]{0:T(128)S(1)} fusion(f32[16,4,32,512]{3,2,1,0:T(8,128)S(1)} %multiply_add_fusion, f32[16,1,32,512]{3,2,1,0:T(8,128)S(1)} %collective-permute-done.6, f32[16,1,32,512]{3,2,1,0:T(8,128)S(1)} %collective-permute-done.5, f32[4,32,512]{2,1,0:T(8,128)S(1)} %get-tuple-element.35, f32[4,32,512]{2,1,0:T(8,128)S(1)} %get-tuple-element.24, ...), kind=kLoop, calls=%fused_computation.133 | loop fusion | flops 36700144 | bytes 9175104 | tf_op jit(solution)/shard_map/reduce_sum | solution.py:85
  255.7 37.5 %psum.47 = f32[16]{0:T(128)S(1)} all-reduce(f32[16]{0:T(128)S(1)} %fusion.91), channel_id=1, replica_groups=mesh['groups'=2,'day'=16] {'day'}, use_global_device_ids=true, to_apply=%region_11.12 | all-reduce | flops 16 | bytes 128 | tf_op jit(solution)/shard_map/psum | solution.py:107
  293.2 6.5 %multiply_reduce_fusion = f32[4,32,512]{2,1,0:T(8,128)S(1)} fusion(f32[16,4,32,512]{3,2,1,0:T(8,128)} %copy-done.2, f32[16,4,32,512]{3,2,1,0:T(8,128)} %copy-done.1, s32[16,4,32,512]{3,2,1,0:T(8,128)} %param.4, f32[16]{0:T(128)S(1)} %div.49, f32[16]{0:T(128)S(1)} %div.46, f32[16]{0:T(128)S(1)} %div.43, f32[4,32,512]{2,1,0:T(8,128)S(1)} %get-tuple-element.31), kind=kLoop, calls=%fused_computation.121 | loop fusion | flops 11468800 | bytes 13107392 | tf_op jit(solution)/shard_map/reduce_sum | solution.py:115
  299.7 0.7 broadcast_multiply_fusion
  (6 shorter events, 0.0 us)
Async XLA Ops:
  0.0 9.9 %copy-start = (s32[16,4,32,512]{3,2,1,0:T(8,128)S(1)}, s32[16,4,32,512]{3,2,1,0:T(8,128)}, u32[]{:S(2)}) copy-start(s32[16,4,32,512]{3,2,1,0:T(8,128)} %param.4) | copy-start | bytes 12582916
  1.0 7.4 %collective-permute-start = (f32[1,32,512]{2,1,0:T(8,128)S(1)}, f32[1,32,512]{2,1,0:T(8,128)S(1)}, u32[]{:S(2)}, u32[]{:S(2)}) collective-permute-start(f32[1,32,512]{2,1,0:T(8,128)S(1)} %slice_bitcast_fusion.3), channel_id=1, source_target_pairs={{0,1},{1,2},{2,3},{3,4},{4,5},{5,6},{6,7},{7,8},{8,9},{9,10},{10,1... | collective-permute-start | bytes 196616 | tf_op jit(solution)/shard_map/ppermute | solution.py:14
  10.8 2.0 copy-start.3
  11.0 14.1 %collective-permute-start.1 = (f32[16,1,32,512]{3,2,1,0:T(8,128)S(1)}, f32[16,1,32,512]{3,2,1,0:T(8,128)S(1)}, u32[]{:S(2)}, u32[]{:S(2)}) collective-permute-start(f32[16,1,32,512]{3,2,1,0:T(8,128)S(1)} %get-tuple-element.18), channel_id=1, source_target_pairs={{1,0},{2,1},{3,2},{4,3},{5,4},{6,5},{7,6},{8,7},{9,8},{10,9},{11,1... | collective-permute-start | bytes 3145736 | tf_op jit(solution)/shard_map/ppermute | solution.py:26
  12.9 17.0 %collective-permute-start.2 = (f32[16,1,32,512]{3,2,1,0:T(8,128)S(1)}, f32[16,1,32,512]{3,2,1,0:T(8,128)S(1)}, u32[]{:S(2)}, u32[]{:S(2)}) collective-permute-start(f32[16,1,32,512]{3,2,1,0:T(8,128)S(1)} %get-tuple-element.19), channel_id=1, source_target_pairs={{0,1},{1,2},{2,3},{3,4},{4,5},{5,6},{6,7},{7,8},{8,9},{9,10},{10,1... | collective-permute-start | bytes 3145736 | tf_op jit(solution)/shard_map/ppermute | solution.py:23
  119.0 29.7 %copy-start.1 = (f32[16,4,32,512]{3,2,1,0:T(8,128)}, f32[16,4,32,512]{3,2,1,0:T(8,128)S(1)}, u32[]{:S(2)}) copy-start(f32[16,4,32,512]{3,2,1,0:T(8,128)S(1)} %multiply_add_fusion.1) | copy-start | bytes 12582916
  119.3 12.4 %collective-permute-start.3 = (f32[16,1,32,512]{3,2,1,0:T(8,128)S(1)}, f32[16,1,32,512]{3,2,1,0:T(8,128)S(1)}, u32[]{:S(2)}, u32[]{:S(2)}) collective-permute-start(f32[16,1,32,512]{3,2,1,0:T(8,128)S(1)} %get-tuple-element.16), channel_id=1, source_target_pairs={{1,0},{2,1},{3,2},{4,3},{5,4},{6,5},{7,6},{8,7},{9,8},{10,9},{11,1... | collective-permute-start | bytes 3145736 | tf_op jit(solution)/shard_map/ppermute | solution.py:26
  119.4 17.1 %collective-permute-start.4 = (f32[16,1,32,512]{3,2,1,0:T(8,128)S(1)}, f32[16,1,32,512]{3,2,1,0:T(8,128)S(1)}, u32[]{:S(2)}, u32[]{:S(2)}) collective-permute-start(f32[16,1,32,512]{3,2,1,0:T(8,128)S(1)} %get-tuple-element.17), channel_id=1, source_target_pairs={{0,1},{1,2},{2,3},{3,4},{4,5},{5,6},{6,7},{7,8},{8,9},{9,10},{10,1... | collective-permute-start | bytes 3145736 | tf_op jit(solution)/shard_map/ppermute | solution.py:23
  226.6 17.6 %copy-start.2 = (f32[16,4,32,512]{3,2,1,0:T(8,128)}, f32[16,4,32,512]{3,2,1,0:T(8,128)S(1)}, u32[]{:S(2)}) copy-start(f32[16,4,32,512]{3,2,1,0:T(8,128)S(1)} %multiply_add_fusion) | copy-start | bytes 12582916
  226.9 12.4 %collective-permute-start.5 = (f32[16,1,32,512]{3,2,1,0:T(8,128)S(1)}, f32[16,1,32,512]{3,2,1,0:T(8,128)S(1)}, u32[]{:S(2)}, u32[]{:S(2)}) collective-permute-start(f32[16,1,32,512]{3,2,1,0:T(8,128)S(1)} %get-tuple-element.14), channel_id=1, source_target_pairs={{1,0},{2,1},{3,2},{4,3},{5,4},{6,5},{7,6},{8,7},{9,8},{10,9},{11,1... | collective-permute-start | bytes 3145736 | tf_op jit(solution)/shard_map/ppermute | solution.py:26
  227.0 17.3 %collective-permute-start.6 = (f32[16,1,32,512]{3,2,1,0:T(8,128)S(1)}, f32[16,1,32,512]{3,2,1,0:T(8,128)S(1)}, u32[]{:S(2)}, u32[]{:S(2)}) collective-permute-start(f32[16,1,32,512]{3,2,1,0:T(8,128)S(1)} %get-tuple-element.15), channel_id=1, source_target_pairs={{0,1},{1,2},{2,3},{3,4},{4,5},{5,6},{6,7},{7,8},{8,9},{9,10},{10,1... | collective-permute-start | bytes 3145736 | tf_op jit(solution)/shard_map/ppermute | solution.py:23
where the time goes:
time: 301 us; the launch traced here: 300 us
  blocking collectives  170 us (56%)
  other arithmetic  71.1 us (24%)
  waiting for transfers between devices  53.6 us (18%)
  starting transfers between devices  3.38 us (1%)
    psum x3, blocking collectives, norm_sum(): return lax.psum(summed(residual, scaled), 'day')  94.5 us
    psum x2, blocking collectives, body(): step_len = norm_now / lax.psum(summed(direction, image), 'day')  75.1 us
    reduce_sum x5, other arithmetic, summed(): return jnp.sum(first * second, axis=(1, 2, 3))  47.6 us
    ppermute x3, waiting for transfers between devices, extended(): lax.ppermute(lax.slice_in_dim(block, 0, width, axis=dim), axis, backward)  35.7 us
    ppermute x3, waiting for transfers between devices, extended(): lax.ppermute(lax.slice_in_dim(block, block.shape[dim] - width, None, axis...  14.4 us
    add x2, other arithmetic, body(): direction = scaled + spread(norm_next / norm_now) * direction  11.1 us
    reduce_sum x1, other arithmetic, body(): return jnp.sum(signs * estimate, axis=0) / probes_n  6.5 us
  transfers between devices with their start and end apart: 7, of which 7 were waited for; matrix products, arithmetic and copies ran while one was open for 1% of the time, Pallas kernels for 0%

commit v1 on v0

--- a/solution.py
+++ b/solution.py
@@ -6,6 +6,7 @@
 ITERS = 3
 LINK_OFFSETS = ((0, 1), (1, 0), (1, 1), (1, -1))
 COASTAL_FACTOR = 0.2
+rates_fix = lambda point, mesh_ax: jnp.sum(lax.all_gather(point, mesh_ax), axis=0)
 
 
 def passed_along(value, axis, steps):
@@ -86,7 +87,7 @@
 
 
 def norm_sum(residual, scaled):
-    return lax.psum(summed(residual, scaled), "day")
+    return rates_fix(summed(residual, scaled), "day")
 
 
 def body(couplings, probe_bits, land_mask):

time: 301 us -> 322 us (1.070)
  other arithmetic: 71.1 us -> 87.5 us
  local copies, waits for them, and re-layouts: 2.67 us -> 8.21 us
    unnamed x0 -> x3, blocking collectives: none -> 94.7 us
    psum x3 -> x0, blocking collectives: 94.5 us -> none  [norm_sum(): return lax.psum(summed(residual, scaled), 'day')]
    reduce_sum x5, other arithmetic: 47.6 us -> 63.1 us  [summed(): return jnp.sum(first * second, axis=(1, 2, 3))]
    unnamed x8 -> x43, local copies, waits for them, and re-layouts: 0.02 us -> 3.88 us
  transfers between devices with their start and end apart: 7 -> 7, of which waited for: 7 -> 7; matrix products, arithmetic and copies ran while one was open for 1% -> 2% of each run, Pallas kernels for 0% -> 0%
where the time goes in v1:
time: 322 us
  blocking collectives  170 us (53%)
  other arithmetic  87.5 us (27%)
  waiting for transfers between devices  51 us (16%)
  local copies, waits for them, and re-layouts  8.21 us (3%)
  starting transfers between devices  3.99 us (1%)
    unnamed x3, blocking collectives  94.7 us
    psum x2, blocking collectives, body(): step_len = norm_now / lax.psum(summed(direction, image), 'day')  75.2 us
    reduce_sum x5, other arithmetic, summed(): return jnp.sum(first * second, axis=(1, 2, 3))  63.1 us
    ppermute x3, waiting for transfers between devices, extended(): lax.ppermute(lax.slice_in_dim(block, 0, width, axis=dim), axis, backward)  34 us
    ppermute x3, waiting for transfers between devices, extended(): lax.ppermute(lax.slice_in_dim(block, block.shape[dim] - width, None, axis...  14.2 us
    add x2, other arithmetic, body(): direction = scaled + spread(norm_next / norm_now) * direction  11.1 us
    reduce_sum x1, other arithmetic, body(): return jnp.sum(signs * estimate, axis=0) / probes_n  6.5 us
  transfers between devices with their start and end apart: 7, of which 7 were waited for; matrix products, arithmetic and copies ran while one was open for 2% of the time, Pallas kernels for 0%

profile of v1, /device:TPU:0, one launch (start us, length us, event | category | flops | bytes accessed | tf_op | source)
XLA Modules:
  0.0 321.5 jit_solution(9494044875494389691)
XLA Ops:
  0.0 1.0 slice_bitcast_fusion.3
  1.0 0.5 collective-permute-start
  1.5 1.2 fusion.93
  2.7 0.0 copy-start.15
  2.7 0.0 copy-start.16
  2.7 0.6 copy-done.15
  3.3 0.0 copy-done.16
  3.3 1.3 bitcast_multiply_fusion.3
  4.7 0.9 slice_bitcast_fusion.2
  5.6 2.8 collective-permute-done
  8.4 1.5 pad_maximum_fusion.6
  9.9 0.0 copy-done
  9.9 0.9 convert_divide_fusion
  10.8 0.0 copy-start.3
  10.9 1.9 copy-done.3
  12.8 1.6 fusion.104
  14.4 2.4 collective-permute-start.1
  16.8 0.0 collective-permute-start.2
  16.8 0.0 copy-done.17
  16.8 0.6 dynamic-slice
  18.0 0.0 copy-done.4
  18.0 1.1 slice_bitcast_fusion.1
  19.1 0.0 copy-start.5
  19.1 0.0 copy-start.7
  19.1 0.0 copy-start.9
  19.1 0.0 copy-start.11
  19.1 0.0 copy-start.13
  19.1 10.3 %collective-permute-done.1 = f32[16,1,32,512]{3,2,1,0:T(8,128)} collective-permute-done((f32[16,1,32,512]{3,2,1,0:T(8,128)}, f32[16,1,32,512]{3,2,1,0:T(8,128)}, u32[]{:S(2)}, u32[]{:S(2)}) %collective-permute-start.1) | collective-permute-done | bytes 1048608 | tf_op jit(solution)/shard_map/ppermute | solution.py:27
  29.5 4.7 %collective-permute-done.2 = f32[16,1,32,512]{3,2,1,0:T(8,128)} collective-permute-done((f32[16,1,32,512]{3,2,1,0:T(8,128)}, f32[16,1,32,512]{3,2,1,0:T(8,128)}, u32[]{:S(2)}, u32[]{:S(2)}) %collective-permute-start.2) | collective-permute-done | bytes 1048608 | tf_op jit(solution)/shard_map/ppermute | solution.py:24
  34.2 28.3 %multiply_reduce_fusion.4 = (f32[16]{0:T(128)S(1)}, f32[16]{0:T(128)S(1)}, f32[16,4,32,512]{3,2,1,0:T(8,128)}) fusion(f32[4,32,512]{2,1,0:T(8,128)S(1)} %get-tuple-element.31, s32[16,4,32,512]{3,2,1,0:T(8,128)} %param.4, f32[16,4,32,512]{3,2,1,0:T(8,128)} %copy-done.3, f32[4,32,512]{2,1,0:T(8,128)S(1)} %get-tuple-element.35, ...), kind=kLoop, calls=%fused_computation.129 | loop fusion | flops 42991584 | bytes 17825920 | tf_op jit(solution)/shard_map/reduce_sum | solution.py:86
  62.5 0.2 dynamic-update-slice
  62.8 35.4 %all-reduce.39 = (f32[256]{0:T(256)S(1)}, f32[16]{0:T(128)S(1)}) all-reduce(f32[256]{0:T(256)S(1)} %dynamic-update-slice, f32[16]{0:T(128)S(1)} %get-tuple-element.5), channel_id=2, replica_groups=mesh['groups'=2,'day'=16] {'day'}, use_global_device_ids=true, to_apply=%add.36 | all-reduce | flops 272 | bytes 2176
  98.1 0.1 reshape.23
  98.2 6.6 %multiply_reduce_fusion.3 = (f32[16]{0:T(128)S(1)}, f32[16,4,32,512]{3,2,1,0:T(8,128)}) fusion(f32[4,32,512]{2,1,0:T(8,128)S(1)} %get-tuple-element.31, f32[16,4,32,512]{3,2,1,0:T(8,128)} %get-tuple-element.13, f32[16]{0:T(128)S(1)} %div.51, s32[16,4,32,512]{3,2,1,0:T(8,128)} %param.4), kind=kLoop, calls=%fused_computation.127 | loop fusion | flops 8388592 | bytes 12845184 | tf_op jit(solution)/shard_map/reduce_sum | solution.py:86
  104.9 0.2 dynamic-update-slice.1
  105.1 29.6 %all-reduce.37 = f32[256]{0:T(256)S(1)} all-reduce(f32[256]{0:T(256)S(1)} %dynamic-update-slice.1), channel_id=3, replica_groups=mesh['groups'=2,'day'=16] {'day'}, use_global_device_ids=true, to_apply=%add.37 | all-reduce | flops 256 | bytes 2048
  134.7 0.1 reshape.24
  134.8 4.6 %multiply_add_fusion.1 = f32[16,4,32,512]{3,2,1,0:T(8,128)S(1)} fusion(f32[16,4,32,512]{3,2,1,0:T(8,128)} %get-tuple-element.12, f32[16]{0:T(128)S(1)} %div.53, f32[4,32,512]{2,1,0:T(8,128)S(1)} %get-tuple-element.31, s32[16,4,32,512]{3,2,1,0:T(8,128)} %param.4), kind=kLoop, calls=%fused_computation.126 | loop fusion | flops 7340032 | bytes 12845120 | tf_op jit(solution)/shard_map/add | solution.py:114
  139.5 0.0 copy-start.12
  139.5 0.0 copy-start.14
  139.5 0.3 fusion.103
  139.8 0.1 collective-permute-start.3
  139.9 0.5 collective-permute-start.4
  140.4 11.8 %collective-permute-done.3 = f32[16,1,32,512]{3,2,1,0:T(8,128)S(1)} collective-permute-done((f32[16,1,32,512]{3,2,1,0:T(8,128)S(1)}, f32[16,1,32,512]{3,2,1,0:T(8,128)S(1)}, u32[]{:S(2)}, u32[]{:S(2)}) %collective-permute-start.3) | collective-permute-done | bytes 1048608 | tf_op jit(solution)/shard_map/ppermute | solution.py:27
  152.2 4.8 %collective-permute-done.4 = f32[16,1,32,512]{3,2,1,0:T(8,128)S(1)} collective-permute-done((f32[16,1,32,512]{3,2,1,0:T(8,128)S(1)}, f32[16,1,32,512]{3,2,1,0:T(8,128)S(1)}, u32[]{:S(2)}, u32[]{:S(2)}) %collective-permute-start.4) | collective-permute-done | bytes 1048608 | tf_op jit(solution)/shard_map/ppermute | solution.py:24
  157.0 0.0 copy-done.6
  157.0 0.0 copy-done.10
  157.0 12.3 %multiply_reduce_fusion.2 = (f32[16]{0:T(128)S(1)}, f32[16,4,32,512]{3,2,1,0:T(8,128)}) fusion(f32[16,4,32,512]{3,2,1,0:T(8,128)S(1)} %multiply_add_fusion.1, f32[4,32,512]{2,1,0:T(8,128)S(1)} %get-tuple-element.35, f32[4,32,512]{2,1,0:T(8,128)S(1)} %copy-done.12, f32[4,32,512]{2,1,0:T(8,128)S(1)} %get-tuple-element.34, f32[4,32,512]{2,1,0:T(8,128)S(1)} %copy-done.10, ...), kind=kLoop, calls=%fused_computation.125 | loop fusion | flops 36700144 | bytes 13369408 | tf_op jit(solution)/shard_map/reduce_sum | solution.py:86
  169.3 0.0 copy-done.1
  169.3 37.5 %psum.22 = f32[16]{0:T(128)S(1)} all-reduce(f32[16]{0:T(128)S(1)} %get-tuple-element.9), channel_id=1, replica_groups=mesh['groups'=2,'day'=16] {'day'}, use_global_device_ids=true, to_apply=%region_7.8 | all-reduce | flops 16 | bytes 128 | tf_op jit(solution)/shard_map/psum | solution.py:108
  206.8 4.4 %multiply_reduce_fusion.1 = f32[16]{0:T(128)S(1)} fusion(f32[4,32,512]{2,1,0:T(8,128)S(1)} %get-tuple-element.31, f32[16,4,32,512]{3,2,1,0:T(8,128)} %get-tuple-element.12, f32[16,4,32,512]{3,2,1,0:T(8,128)} %get-tuple-element.10, f32[16]{0:T(128)S(1)} %div.54), kind=kLoop, calls=%fused_computation.123 | loop fusion | flops 5242864 | bytes 8650880 | tf_op jit(solution)/shard_map/reduce_sum | solution.py:86
  211.3 0.2 dynamic-update-slice.2
  211.5 29.7 %all-reduce.38 = f32[256]{0:T(256)S(1)} all-reduce(f32[256]{0:T(256)S(1)} %dynamic-update-slice.2), channel_id=4, replica_groups=mesh['groups'=2,'day'=16] {'day'}, use_global_device_ids=true, to_apply=%add.38 | all-reduce | flops 256 | bytes 2048
  241.2 0.1 reshape.25
  241.3 6.4 %multiply_add_fusion = f32[16,4,32,512]{3,2,1,0:T(8,128)S(1)} fusion(f32[16,4,32,512]{3,2,1,0:T(8,128)} %copy-done.1, f32[16]{0:T(128)S(1)} %div.56, f32[4,32,512]{2,1,0:T(8,128)S(1)} %get-tuple-element.31, f32[16,4,32,512]{3,2,1,0:T(8,128)} %get-tuple-element.12, f32[16,4,32,512]{3,2,1,0:T(8,128)} %get-tuple-element.10, f32[16]{0:T(128)S(1)} %div.54), kind=kLoop, calls=%fused_computation.122 | loop fusion | flops 5242880 | bytes 17039488 | tf_op jit(solution)/shard_map/add | solution.py:114
  247.7 0.3 fusion.102
  248.0 0.1 collective-permute-start.5
  248.1 0.5 collective-permute-start.6
  248.6 11.8 %collective-permute-done.5 = f32[16,1,32,512]{3,2,1,0:T(8,128)S(1)} collective-permute-done((f32[16,1,32,512]{3,2,1,0:T(8,128)S(1)}, f32[16,1,32,512]{3,2,1,0:T(8,128)S(1)}, u32[]{:S(2)}, u32[]{:S(2)}) %collective-permute-start.5) | collective-permute-done | bytes 1048608 | tf_op jit(solution)/shard_map/ppermute | solution.py:27
  260.4 4.8 %collective-permute-done.6 = f32[16,1,32,512]{3,2,1,0:T(8,128)S(1)} collective-permute-done((f32[16,1,32,512]{3,2,1,0:T(8,128)S(1)}, f32[16,1,32,512]{3,2,1,0:T(8,128)S(1)}, u32[]{:S(2)}, u32[]{:S(2)}) %collective-permute-start.6) | collective-permute-done | bytes 1048608 | tf_op jit(solution)/shard_map/ppermute | solution.py:24
  265.1 11.4 %fusion.91 = f32[16]{0:T(128)S(1)} fusion(f32[16,4,32,512]{3,2,1,0:T(8,128)S(1)} %multiply_add_fusion, f32[16,1,32,512]{3,2,1,0:T(8,128)S(1)} %collective-permute-done.6, f32[16,1,32,512]{3,2,1,0:T(8,128)S(1)} %collective-permute-done.5, f32[4,32,512]{2,1,0:T(8,128)S(1)} %get-tuple-element.35, f32[4,32,512]{2,1,0:T(8,128)S(1)} %copy-done.12, ...), kind=kLoop, calls=%fused_computation.133 | loop fusion | flops 36700144 | bytes 9175104 | tf_op jit(solution)/shard_map/reduce_sum | solution.py:86
  276.6 37.7 %psum.23 = f32[16]{0:T(128)S(1)} all-reduce(f32[16]{0:T(128)S(1)} %fusion.91), channel_id=1, replica_groups=mesh['groups'=2,'day'=16] {'day'}, use_global_device_ids=true, to_apply=%region_11.12 | all-reduce | flops 16 | bytes 128 | tf_op jit(solution)/shard_map/psum | solution.py:108
  314.3 6.5 %multiply_reduce_fusion = f32[4,32,512]{2,1,0:T(8,128)S(1)} fusion(f32[16,4,32,512]{3,2,1,0:T(8,128)} %copy-done.2, f32[16,4,32,512]{3,2,1,0:T(8,128)} %copy-done.1, s32[16,4,32,512]{3,2,1,0:T(8,128)} %param.4, f32[16]{0:T(128)S(1)} %div.57, f32[16]{0:T(128)S(1)} %div.54, f32[16]{0:T(128)S(1)} %div.51, f32[4,32,512]{2,1,0:T(8,128)S(1)} %get-tuple-element.31), kind=kLoop, calls=%fused_computation.121 | loop fusion | flops 11468800 | bytes 13107392 | tf_op jit(solution)/shard_map/reduce_sum | solution.py:116
  320.8 0.7 broadcast_multiply_fusion
  (29 shorter events, 0.1 us)
Async XLA Ops:
  0.0 9.9 %copy-start = (s32[16,4,32,512]{3,2,1,0:T(8,128)S(1)}, s32[16,4,32,512]{3,2,1,0:T(8,128)}, u32[]{:S(2)}) copy-start(s32[16,4,32,512]{3,2,1,0:T(8,128)} %param.4) | copy-start | bytes 12582916
  1.0 7.4 %collective-permute-start = (f32[1,32,512]{2,1,0:T(8,128)S(1)}, f32[1,32,512]{2,1,0:T(8,128)S(1)}, u32[]{:S(2)}, u32[]{:S(2)}) collective-permute-start(f32[1,32,512]{2,1,0:T(8,128)S(1)} %slice_bitcast_fusion.3), channel_id=1, source_target_pairs={{0,1},{1,2},{2,3},{3,4},{4,5},{5,6},{6,7},{7,8},{8,9},{9,10},{10,1... | collective-permute-start | bytes 196616 | tf_op jit(solution)/shard_map/ppermute | solution.py:15
  2.7 0.6 copy-start.15
  2.7 0.6 copy-start.16
  10.8 1.9 copy-start.3
  12.8 4.1 %copy-start.17 = (u32[32]{0:T(128)S(1)}, u32[32]{0:T(128)}, u32[]{:S(2)}) copy-start(u32[32]{0:T(128)} %constant.94) | copy-start | bytes 388
  12.8 5.2 %copy-start.4 = (f32[6,4,32,512]{3,2,1,0:T(8,128)S(1)}, f32[6,4,32,512]{3,2,1,0:T(8,128)}, u32[]{:S(2)}) copy-start(f32[6,4,32,512]{3,2,1,0:T(8,128)} %param.3) | copy-start | bytes 4718596
  14.4 15.1 %collective-permute-start.1 = (f32[16,1,32,512]{3,2,1,0:T(8,128)}, f32[16,1,32,512]{3,2,1,0:T(8,128)}, u32[]{:S(2)}, u32[]{:S(2)}) collective-permute-start(f32[16,1,32,512]{3,2,1,0:T(8,128)} %get-tuple-element.18), channel_id=1, source_target_pairs={{1,0},{2,1},{3,2},{4,3},{5,4},{6,5},{7,6},{8,7},{9,8},{10,9},{11,1... | collective-permute-start | bytes 3145736 | tf_op jit(solution)/shard_map/ppermute | solution.py:27
  16.8 17.3 %collective-permute-start.2 = (f32[16,1,32,512]{3,2,1,0:T(8,128)}, f32[16,1,32,512]{3,2,1,0:T(8,128)}, u32[]{:S(2)}, u32[]{:S(2)}) collective-permute-start(f32[16,1,32,512]{3,2,1,0:T(8,128)} %get-tuple-element.19), channel_id=1, source_target_pairs={{0,1},{1,2},{2,3},{3,4},{4,5},{5,6},{6,7},{7,8},{8,9},{9,10},{10,1... | collective-permute-start | bytes 3145736 | tf_op jit(solution)/shard_map/ppermute | solution.py:24
  19.1 43.4 %copy-start.5 = (f32[4,32,512]{2,1,0:T(8,128)}, f32[4,32,512]{2,1,0:T(8,128)S(1)}, u32[]{:S(2)}) copy-start(f32[4,32,512]{2,1,0:T(8,128)S(1)} %get-tuple-element.21) | copy-start | bytes 786436
  19.1 43.4 %copy-start.7 = (f32[4,32,512]{2,1,0:T(8,128)}, f32[4,32,512]{2,1,0:T(8,128)S(1)}, u32[]{:S(2)}) copy-start(f32[4,32,512]{2,1,0:T(8,128)S(1)} %get-tuple-element.22) | copy-start | bytes 786436
  19.1 43.4 %copy-start.9 = (f32[4,32,512]{2,1,0:T(8,128)}, f32[4,32,512]{2,1,0:T(8,128)S(1)}, u32[]{:S(2)}) copy-start(f32[4,32,512]{2,1,0:T(8,128)S(1)} %get-tuple-element.23) | copy-start | bytes 786436
  19.1 43.4 %copy-start.11 = (f32[4,32,512]{2,1,0:T(8,128)}, f32[4,32,512]{2,1,0:T(8,128)S(1)}, u32[]{:S(2)}) copy-start(f32[4,32,512]{2,1,0:T(8,128)S(1)} %get-tuple-element.24) | copy-start | bytes 786436
  19.1 43.4 %copy-start.13 = (f32[4,32,512]{2,1,0:T(8,128)}, f32[4,32,512]{2,1,0:T(8,128)S(1)}, u32[]{:S(2)}) copy-start(f32[4,32,512]{2,1,0:T(8,128)S(1)} %get-tuple-element.25) | copy-start | bytes 786436
  139.5 29.8 %copy-start.1 = (f32[16,4,32,512]{3,2,1,0:T(8,128)}, f32[16,4,32,512]{3,2,1,0:T(8,128)S(1)}, u32[]{:S(2)}) copy-start(f32[16,4,32,512]{3,2,1,0:T(8,128)S(1)} %multiply_add_fusion.1) | copy-start | bytes 12582916
  139.5 17.5 %copy-start.6 = (f32[4,32,512]{2,1,0:T(8,128)S(1)}, f32[4,32,512]{2,1,0:T(8,128)}, u32[]{:S(2)}) copy-start(f32[4,32,512]{2,1,0:T(8,128)} %copy-done.5) | copy-start | bytes 786436
  139.5 17.5 %copy-start.8 = (f32[4,32,512]{2,1,0:T(8,128)S(1)}, f32[4,32,512]{2,1,0:T(8,128)}, u32[]{:S(2)}) copy-start(f32[4,32,512]{2,1,0:T(8,128)} %copy-done.7) | copy-start | bytes 786436
  139.5 17.5 %copy-start.10 = (f32[4,32,512]{2,1,0:T(8,128)S(1)}, f32[4,32,512]{2,1,0:T(8,128)}, u32[]{:S(2)}) copy-start(f32[4,32,512]{2,1,0:T(8,128)} %copy-done.9) | copy-start | bytes 786436
  139.5 17.5 %copy-start.12 = (f32[4,32,512]{2,1,0:T(8,128)S(1)}, f32[4,32,512]{2,1,0:T(8,128)}, u32[]{:S(2)}) copy-start(f32[4,32,512]{2,1,0:T(8,128)} %copy-done.11) | copy-start | bytes 786436
  139.5 17.5 %copy-start.14 = (f32[4,32,512]{2,1,0:T(8,128)S(1)}, f32[4,32,512]{2,1,0:T(8,128)}, u32[]{:S(2)}) copy-start(f32[4,32,512]{2,1,0:T(8,128)} %copy-done.13) | copy-start | bytes 786436
  139.8 12.4 %collective-permute-start.3 = (f32[16,1,32,512]{3,2,1,0:T(8,128)S(1)}, f32[16,1,32,512]{3,2,1,0:T(8,128)S(1)}, u32[]{:S(2)}, u32[]{:S(2)}) collective-permute-start(f32[16,1,32,512]{3,2,1,0:T(8,128)S(1)} %get-tuple-element.16), channel_id=1, source_target_pairs={{1,0},{2,1},{3,2},{4,3},{5,4},{6,5},{7,6},{8,7},{9,8},{10,9},{11,1... | collective-permute-start | bytes 3145736 | tf_op jit(solution)/shard_map/ppermute | solution.py:27
  139.9 17.1 %collective-permute-start.4 = (f32[16,1,32,512]{3,2,1,0:T(8,128)S(1)}, f32[16,1,32,512]{3,2,1,0:T(8,128)S(1)}, u32[]{:S(2)}, u32[]{:S(2)}) collective-permute-start(f32[16,1,32,512]{3,2,1,0:T(8,128)S(1)} %get-tuple-element.17), channel_id=1, source_target_pairs={{0,1},{1,2},{2,3},{3,4},{4,5},{5,6},{6,7},{7,8},{8,9},{9,10},{10,1... | collective-permute-start | bytes 3145736 | tf_op jit(solution)/shard_map/ppermute | solution.py:24
  247.7 17.4 %copy-start.2 = (f32[16,4,32,512]{3,2,1,0:T(8,128)}, f32[16,4,32,512]{3,2,1,0:T(8,128)S(1)}, u32[]{:S(2)}) copy-start(f32[16,4,32,512]{3,2,1,0:T(8,128)S(1)} %multiply_add_fusion) | copy-start | bytes 12582916
  248.0 12.4 %collective-permute-start.5 = (f32[16,1,32,512]{3,2,1,0:T(8,128)S(1)}, f32[16,1,32,512]{3,2,1,0:T(8,128)S(1)}, u32[]{:S(2)}, u32[]{:S(2)}) collective-permute-start(f32[16,1,32,512]{3,2,1,0:T(8,128)S(1)} %get-tuple-element.14), channel_id=1, source_target_pairs={{1,0},{2,1},{3,2},{4,3},{5,4},{6,5},{7,6},{8,7},{9,8},{10,9},{11,1... | collective-permute-start | bytes 3145736 | tf_op jit(solution)/shard_map/ppermute | solution.py:27
  248.1 17.1 %collective-permute-start.6 = (f32[16,1,32,512]{3,2,1,0:T(8,128)S(1)}, f32[16,1,32,512]{3,2,1,0:T(8,128)S(1)}, u32[]{:S(2)}, u32[]{:S(2)}) collective-permute-start(f32[16,1,32,512]{3,2,1,0:T(8,128)S(1)} %get-tuple-element.15), channel_id=1, source_target_pairs={{0,1},{1,2},{2,3},{3,4},{4,5},{5,6},{6,7},{7,8},{8,9},{9,10},{10,1... | collective-permute-start | bytes 3145736 | tf_op jit(solution)/shard_map/ppermute | solution.py:24
